TPU v7x, 32 devices: a whole 2x2x4 slice. The times are simulated.
32 devices in a mesh: aux: 8 (over z, core), orb: 2 (over y), rep: 2 (over x).
Axes of the slice: x: 2, y: 2, z: 4, core: 2. Of those that a mesh axis runs over, the one named last changes fastest.
Arguments:
- slab: bfloat16 [4096, 4, 1024], P('aux', None, 'orb'), may hold values from -6 to 6
- occ_density: bfloat16 [1024, 512], P('orb'), may hold values from -0.25 to 0.25
- virt_density: bfloat16 [1024, 512], P('orb'), may hold values from -0.25 to 0.25
- block_mask: int32 [32, 8], P('aux', 'orb'), may hold values 0 or 1
- matching: int32 [2, 8], replicated, may hold values from 0 to 7, as said below
Outputs:
- chi_pair: float32 [2, 4096, 512], P('rep', ('aux', 'orb'))
- chi_self: float32 [4096, 512], P(('aux', 'orb'), 'rep')
Inputs may be any that keep to these rules, and one draw needn't show every extreme that they name: `matching`: each row pairs the 8 owners: entry p names the partner of p, the partner's entry names p, and no owner is its own partner.
All inputs are finite; a program needn't handle non-finite values. No bound on the sum of `block_mask` on one device may be relied on, other than what follows from the above.
Results may differ from a plain program's by a relative error of at most 0.0041.
Values may be sent and summed in bfloat16 or wider, within the bound.
A program may use at most 64 MiB of HBM per device.

v0:
```python
import functools
import math

import jax
import jax.numpy as jnp
from jax import lax
from jax.experimental import pallas as pl
from jax.experimental.pallas import tpu as pltpu
from jax.sharding import PartitionSpec as P

BLOCK = 128
MESH = pl.DeviceIdType.MESH
CONTRACT = (((1,), (1,)), ((), ()))


def kernel(sizes, factor, match_ref, masked, occ_dens, virt_dens, pair_out, self_out, *scratch):
    chips, orbs, reps, pieces, groups, rows_piece, half = sizes
    gath = scratch[:pieces]
    (occ, parts, whole, arrived, ends, landed, self_tile, self_arrived,
     recv_sem, up_sem, down_sem, core_send, core_recv, local_sem, end_send, end_recv,
     part_send, part_recv, self_send, self_recv) = scratch[pieces:]
    per_group = pieces // groups
    cols_group = per_group * rows_piece
    batch, aux_rows, orb_cols = masked.shape
    rows_out = aux_rows // orbs
    self_cols = aux_rows // reps

    a = lax.axis_index("aux")
    o = lax.axis_index("orb")
    r = lax.axis_index("rep")
    z = a // 2
    k = a % 2

    def peer(j):
        to_orb, to_rep = (o + j // reps) % orbs, (r + j % reps) % reps
        return to_orb, to_rep, {"orb": to_orb, "rep": to_rep}

    inner = jnp.logical_and(z >= 1, z <= chips - 2)
    at_end = jnp.logical_or(z == 0, z == chips - 1)
    up_ok = z + 1 <= chips - 2
    down_ok = z - 1 >= 1
    feeds = jnp.logical_or(z == 1, z == chips - 2)
    end_aux = jnp.where(z == 1, k, 2 * (chips - 1) + k)

    barrier = pltpu.get_barrier_semaphore()

    @pl.when(z > 0)
    def _():
        pl.semaphore_signal(barrier, inc=1, device_id={"aux": a - 2}, device_id_type=MESH)

    @pl.when(z < chips - 1)
    def _():
        pl.semaphore_signal(barrier, inc=1, device_id={"aux": a + 2}, device_id_type=MESH)

    pl.semaphore_signal(barrier, inc=1, device_id={"aux": 2 * z + 1 - k}, device_id_type=MESH)
    for j in range(1, orbs * reps):
        pl.semaphore_signal(barrier, inc=1, device_id=peer(j)[2], device_id_type=MESH)
    pl.semaphore_wait(barrier, orbs * reps + jnp.where(at_end, 1, 2))

    def piece(c):
        return masked.at[pl.ds(r * half, half), pl.ds(c * rows_piece, rows_piece), :]

    def remote(src, dst, send, recv, where):
        return pltpu.make_async_remote_copy(
            src_ref=src, dst_ref=dst, send_sem=send, recv_sem=recv, device_id=where, device_id_type=MESH
        )

    def slot(c, zz):
        return gath[c].at[2 * zz + k]

    def up(c, zz, src):
        return remote(src, slot(c, zz), up_sem.at[c, zz], recv_sem.at[c, zz], {"aux": a + 2})

    def down(c, zz, src):
        return remote(src, slot(c, zz), down_sem.at[c, zz], recv_sem.at[c, zz], {"aux": a - 2})

    def cross(c, zz, src):
        return remote(src, slot(c, zz), core_send.at[c, zz], core_recv.at[c, zz], {"aux": 2 * z + 1 - k})

    def local(c):
        return pltpu.make_async_copy(piece(c), gath[c].at[a], local_sem.at[c])

    def lower(c, send):
        for d in range(1, chips):
            @pl.when(z - d >= 0)
            def _():
                zz = jnp.maximum(z - d, 0)
                up(c, zz, slot(c, zz)).wait_recv()
                if send:
                    up(c, zz, slot(c, zz)).start()
                cross(c, zz, slot(c, zz)).start()

    def upper(c, send):
        for d in range(1, chips):
            @pl.when(z + d <= chips - 1)
            def _():
                zz = jnp.minimum(z + d, chips - 1)
                down(c, zz, slot(c, zz)).wait_recv()
                if send:
                    down(c, zz, slot(c, zz)).start()
                cross(c, zz, slot(c, zz)).start()

    def own(c):
        @pl.when(up_ok)
        def _():
            up(c, z, piece(c)).start()

        @pl.when(down_ok)
        def _():
            down(c, z, piece(c)).start()

        @pl.when(inner)
        def _():
            cross(c, z, piece(c)).start()
            local(c).start()

    def relay(c):
        @pl.when(jnp.logical_and(inner, up_ok))
        def _():
            lower(c, True)

        @pl.when(jnp.logical_and(inner, down_ok))
        def _():
            upper(c, True)

    def complete(c):
        @pl.when(inner)
        def _():
            @pl.when(jnp.logical_not(up_ok))
            def _():
                lower(c, False)

            @pl.when(jnp.logical_not(down_ok))
            def _():
                upper(c, False)

    def part_copy(g, t, j):
        to_orb, to_rep, where = peer(j)
        return remote(parts.at[g, t, to_rep, pl.ds(to_orb * rows_out, rows_out), :], arrived.at[g, t, j - 1],
                      part_send.at[g, t, j - 1], part_recv.at[g, t, j - 1], where)

    def feed(g):
        return remote(ends.at[g], landed.at[g], end_send.at[g], end_recv.at[g], {"aux": end_aux})

    def self_copy(j):
        to_orb = (o + j) % orbs
        return remote(self_tile.at[pl.ds(to_orb * rows_out, rows_out), :], self_arrived.at[j - 1],
                      self_send.at[j - 1], self_recv.at[j - 1], {"orb": to_orb})

    def product(l, rows_l):
        moved = jnp.dot(rows_l, virt_dens[...], preferred_element_type=jnp.float32).astype(jnp.bfloat16)
        return lax.dot_general(occ[l], moved, CONTRACT, preferred_element_type=jnp.float32)

    def end_occ(c):
        @pl.when(feeds)
        def _():
            rows_e = gath[c][end_aux].reshape(half * rows_piece, orb_cols)
            made = jnp.dot(rows_e, occ_dens[...], preferred_element_type=jnp.float32).astype(jnp.bfloat16)
            occ[batch:, c * rows_piece:(c + 1) * rows_piece, :] = made.reshape(half, rows_piece, orb_cols)

    def group(g):
        span = range(g * per_group, (g + 1) * per_group)

        @pl.when(inner)
        def _():
            for c in span:
                for zz in range(chips):
                    remote(gath[c].at[2 * zz + k], gath[c].at[2 * zz + 1 - k], core_send.at[c, zz],
                           core_recv.at[c, zz], {"aux": 2 * z + 1 - k}).wait_recv()
                local(c).wait()

            def one_tile(n, carry):
                t, turn = n // reps, n % reps
                owner = jnp.where(t == 0, a, end_aux)
                first = jnp.where(t == 0, r * half, batch)
                partner = match_ref[turn, owner]
                total = None
                for i in range(half):
                    rows_l = [gath[c][partner, i] for c in span]
                    rows_l = rows_l[0] if per_group == 1 else jnp.concatenate(rows_l, 0)
                    term = product(first + i, rows_l)
                    total = term if total is None else total + term
                total = total * factor
                parts[g, t, turn] = total.astype(jnp.bfloat16)
                whole[g, t, turn] = total
                return carry

            lax.fori_loop(0, jnp.where(feeds, 2 * reps, reps), one_tile, 0)
            for j in range(1, orbs * reps):
                @pl.when(feeds)
                def _():
                    part_copy(g, 1, j).start()
            for j in range(1, orbs * reps):
                part_copy(g, 0, j).start()

    def summed(g, t):
        total = whole[g, t, r, pl.ds(o * rows_out, rows_out), :]
        for j in range(1, orbs * reps):
            part_copy(g, t, j).wait_recv()
            total = total + arrived[g, t, j - 1].astype(jnp.float32)
        return total

    def finish(g):
        @pl.when(inner)
        def _():
            @pl.when(feeds)
            def _():
                ends[g] = summed(g, 1)
                feed(g).start()

            pair_out[:, g * cols_group:(g + 1) * cols_group] = summed(g, 0)

    ahead = min(3, pieces)
    ready = 0
    closed = 0

    def one_occ(l, carry):
        occ[l] = jnp.dot(masked[l], occ_dens[...], preferred_element_type=jnp.float32).astype(jnp.bfloat16)
        return carry

    own(0)
    own(1)
    lax.fori_loop(0, batch, one_occ, 0)
    for c in range(min(ahead, pieces)):
        relay(c)
        end_occ(c)
    for c in range(pieces):
        if c + 2 < pieces:
            own(c + 2)
        if c + ahead < pieces:
            relay(c + ahead)
            end_occ(c + ahead)
        filled = c + ahead >= pieces - 1
        if filled and (ready + 1) * per_group <= c:
            group(ready)
            ready += 1
        complete(c)
        if c == 0:
            total = None
            for l in range(batch):
                term = product(l, masked[l, pl.ds(r * self_cols, self_cols), :])
                total = term if total is None else total + term
            self_tile[...] = total * factor
        if c == 1:
            for j in range(1, orbs):
                self_copy(j).start()
        if filled and c == pieces - 2 and closed + 1 < ready:
            finish(closed)
            closed += 1
        if filled and c < pieces - 1 and (ready + 1) * per_group <= c + 1:
            group(ready)
            ready += 1
    for g in range(ready, groups):
        group(g)
    total = self_tile[pl.ds(o * rows_out, rows_out), :]
    for j in range(1, orbs):
        self_copy(j).wait_recv()
        total = total + self_arrived[j - 1]
    self_out[...] = total
    for g in range(closed, groups):
        finish(g)

    @pl.when(at_end)
    def _():
        for g in range(groups):
            feed(g).wait_recv()
            pair_out[:, g * cols_group:(g + 1) * cols_group] = landed[g]

    for c in range(pieces):
        for d in range(chips):
            @pl.when(jnp.logical_and(up_ok, z - d >= 0))
            def _():
                up(c, jnp.maximum(z - d, 0), piece(c)).wait_send()

            @pl.when(jnp.logical_and(down_ok, z + d <= chips - 1))
            def _():
                down(c, jnp.minimum(z + d, chips - 1), piece(c)).wait_send()

        @pl.when(inner)
        def _():
            for zz in range(chips):
                cross(c, zz, piece(c)).wait_send()

    for j in range(1, orbs):
        self_copy(j).wait_send()
    for g in range(groups):
        @pl.when(inner)
        def _():
            for j in range(1, orbs * reps):
                part_copy(g, 0, j).wait_send()

        @pl.when(feeds)
        def _():
            for j in range(1, orbs * reps):
                part_copy(g, 1, j).wait_send()
            feed(g).wait_send()


def per_device(slab, occ_density, virt_density, block_mask, matching):
    owners = lax.axis_size("aux")
    orbs = lax.axis_size("orb")
    reps = lax.axis_size("rep")
    chips = owners // 2
    aux_rows, batch, orb_cols = slab.shape
    pieces = max(2, 32 // chips)
    rows_piece = aux_rows // pieces
    per_group = max(1, BLOCK // rows_piece)
    groups = pieces // per_group
    cols_group = per_group * rows_piece
    half = batch // reps
    rows_out = aux_rows // orbs
    self_cols = aux_rows // reps
    weights = block_mask.astype(jnp.bfloat16)
    spread = jnp.repeat(jnp.repeat(weights, BLOCK, axis=0), BLOCK, axis=1)
    masked = jnp.transpose(slab, (1, 0, 2)) * spread[None]
    factor = 1.0 / math.sqrt(batch * orb_cols * orbs)
    dma = pltpu.SemaphoreType.DMA
    vmem = pl.BlockSpec(memory_space=pltpu.VMEM)
    bf16, f32 = jnp.bfloat16, jnp.float32
    pair, own = pl.pallas_call(
        functools.partial(kernel, (chips, orbs, reps, pieces, groups, rows_piece, half), factor),
        out_shape=(
            jax.ShapeDtypeStruct((rows_out, aux_rows), f32),
            jax.ShapeDtypeStruct((rows_out, self_cols), f32),
        ),
        in_specs=[pl.BlockSpec(memory_space=pltpu.SMEM), vmem, vmem, vmem],
        out_specs=(vmem, vmem),
        scratch_shapes=[pltpu.VMEM((owners, half, rows_piece, orb_cols), bf16) for _ in range(pieces)] + [
            pltpu.VMEM((batch + half, aux_rows, orb_cols), bf16),
            pltpu.VMEM((groups, 2, reps, aux_rows, cols_group), bf16),
            pltpu.VMEM((groups, 2, reps, aux_rows, cols_group), f32),
            pltpu.VMEM((groups, 2, orbs * reps - 1, rows_out, cols_group), bf16),
            pltpu.VMEM((groups, rows_out, cols_group), f32),
            pltpu.VMEM((groups, rows_out, cols_group), f32),
            pltpu.VMEM((aux_rows, self_cols), f32),
            pltpu.VMEM((orbs - 1, rows_out, self_cols), f32),
            dma((pieces, chips)), dma((pieces, chips)), dma((pieces, chips)),
            dma((pieces, chips)), dma((pieces, chips)),
            dma((pieces,)), dma((groups,)), dma((groups,)),
            dma((groups, 2, orbs * reps - 1)), dma((groups, 2, orbs * reps - 1)),
            dma((orbs - 1,)), dma((orbs - 1,)),
        ],
        compiler_params=pltpu.CompilerParams(
            collective_id=0, has_side_effects=True, vmem_limit_bytes=56 * 2**20
        ),
    )(matching, masked, occ_density, virt_density)
    return (pair[None], own)


def solution(mesh):
    return jax.shard_map(
        per_device,
        mesh=mesh,
        in_specs=(P("aux", None, "orb"), P("orb", None), P("orb", None), P("aux", "orb"), P()),
        out_specs=(P("rep", ("aux", "orb"), None), P(("aux", "orb"), "rep")),
        check_vma=False,
    )
```

profile of v0, /device:TPU:1, one launch (start us, length us, event | category | flops | bytes accessed | tf_op | source)
XLA Modules:
  0.0 78.9 jit_solution(5884213782103787817)
XLA Ops:
  0.6 0.7 convert_element_type.3
  1.3 0.6 broadcast_in_dim.10
  1.9 0.1 copy.13
  2.0 3.7 %fusion.masked = bf16[4,512,512]{2,1,0:T(8,128)(2,1)} fusion(bf16[512,4,512]{2,1,0:T(4,128)(2,1)} %param.5, bf16[512,512]{1,0:T(8,128)(2,1)S(1)} %bitcast.8), kind=kLoop, calls=%fused_computation.1 | loop fusion | flops 1048576 | bytes 4718592 | tf_op jit(solution)/shard_map/mul | solution.py:315
  5.7 69.7 %shard_map.68 = (f32[256,512]{1,0:T(8,128)}, f32[256,256]{1,0:T(8,128)}) custom-call(s32[2,8]{1,0:T(2,128)} %match_ref.1, bf16[4,512,512]{2,1,0:T(8,128)(2,1)} %fusion.masked, bf16[512,512]{1,0:T(8,128)(2,1)} %occ_dens.1, bf16[512,512]{1,0:T(8,128)(2,1)} %virt_dens.1), custom_call_target="tpu_custom_call" | custom-call | tf_op jit(solution)/shard_map/pallas_call | solution.py:320
  75.4 1.9 %copy.16 = f32[1,256,512]{2,1,0:T(8,128)} copy(f32[1,256,512]{2,1,0:T(8,128)} %bitcast.11) | data formatting | bytes 1048576
  77.3 1.7 %copy.17 = f32[256,256]{1,0:T(8,128)} copy(f32[256,256]{1,0:T(8,128)} %get-tuple-element.9) | data formatting | bytes 524288
  (1 shorter events, 0.0 us)
where the time goes:
time: 79.2 us; the launch traced here: 78.9 us
  Pallas kernels  69.7 us (88%)
  other arithmetic  4.36 us (6%)
  local copies, waits for them, and re-layouts  4.24 us (5%)
    pallas_call x1, Pallas kernels, per_device(): pl.pallas_call(functools.partial(kernel, (chips, orbs, reps, pieces, grou...  69.7 us
    mul x1, other arithmetic, per_device(): masked = jnp.transpose(slab, (1, 0, 2)) * spread[None]  3.67 us
    unnamed x3, local copies, waits for them, and re-layouts  3.62 us

commit v1 on v0

v1 whole, which is shorter than its diff:
```python
import functools
import math

import jax
import jax.numpy as jnp
from jax import lax
from jax.experimental import pallas as pl
from jax.experimental.pallas import tpu as pltpu
from jax.sharding import PartitionSpec as P

BLOCK = 128
MESH = pl.DeviceIdType.MESH
CONTRACT = (((1,), (1,)), ((), ()))
F32, BF16 = jnp.float32, jnp.bfloat16


def kernel(sizes, factor, match_ref, mask_ref, slab, occ_hbm, virt_hbm, pair_out, self_out, *scratch):
    chips, orbs, reps, pieces, groups, chunk = sizes
    gath = scratch[:groups]
    (raw, masked, occ_dens, virt_dens, occ, parts, end_parts, whole, arrived, end_arrived,
     self_parts, self_whole, self_arrived, raw_sem, dens_sem, local_sem, send_sem, recv_sem,
     core_send, core_recv, part_send, part_recv, end_send, end_recv, self_send, self_recv) = scratch[groups:]
    half, aux_rows, orb_cols = masked.shape
    rows_piece = aux_rows // pieces
    per_group = pieces // groups
    cols_group = aux_rows // groups
    rows_out = aux_rows // orbs
    self_cols = aux_rows // reps
    peers = orbs * reps

    a = lax.axis_index("aux")
    o = lax.axis_index("orb")
    r = lax.axis_index("rep")
    z = a // 2
    k = a % 2
    inner = jnp.logical_and(z >= 1, z <= chips - 2)
    at_end = jnp.logical_not(inner)
    feeds = jnp.logical_or(z == 1, z == chips - 2)
    end_aux = jnp.where(z == 1, k, 2 * (chips - 1) + k)
    feed_aux = jnp.where(z == 0, 2 + k, 2 * (chips - 2) + k)
    other = 2 * z + 1 - k

    def peer(j):
        to_orb, to_rep = (o + j // reps) % orbs, (r + j % reps) % reps
        return to_orb, {"orb": to_orb, "rep": to_rep}

    def rows(c):
        return pl.ds(c * rows_piece, rows_piece)

    def raw_copy(c):
        return pltpu.make_async_copy(slab.at[rows(c)], raw.at[rows(c)], raw_sem.at[c])

    for c in range(pieces):
        raw_copy(c).start()
    occ_copy = pltpu.make_async_copy(occ_hbm, occ_dens, dens_sem.at[0])
    virt_copy = pltpu.make_async_copy(virt_hbm, virt_dens, dens_sem.at[1])
    occ_copy.start()
    virt_copy.start()

    barrier = pltpu.get_barrier_semaphore()

    def greet(where):
        pl.semaphore_signal(barrier, inc=1, device_id=where, device_id_type=MESH)

    for d in range(1, chips):
        @pl.when(jnp.logical_and(z - d >= 0, jnp.logical_or(inner, z - d >= 1)))
        def _():
            greet({"aux": a - 2 * d})

        @pl.when(jnp.logical_and(z + d <= chips - 1, jnp.logical_or(inner, z + d <= chips - 2)))
        def _():
            greet({"aux": a + 2 * d})

    greet({"aux": other})
    for j in range(1, peers):
        greet(peer(j)[1])

        @pl.when(feeds)
        def _():
            greet(dict(peer(j)[1], aux=end_aux))

        @pl.when(at_end)
        def _():
            greet(dict(peer(j)[1], aux=feed_aux))

    def remote(src, dst, send, recv, where):
        return pltpu.make_async_remote_copy(
            src_ref=src, dst_ref=dst, send_sem=send, recv_sem=recv, device_id=where, device_id_type=MESH
        )

    def piece(c):
        return masked.at[:, rows(c), :]

    def slot(c, owner):
        return gath[c // per_group].at[owner, :, pl.ds(c % per_group * rows_piece, rows_piece), :]

    def direct(c, source, target):
        return remote(piece(c), slot(c, 2 * source + k), send_sem.at[c, target], recv_sem.at[c, source],
                      {"aux": 2 * target + k})

    def cross(c, zz, src):
        return remote(src, slot(c, 2 * zz + k), core_send.at[c, zz], core_recv.at[c, zz], {"aux": other})

    def local(c):
        return pltpu.make_async_copy(piece(c), slot(c, a), local_sem.at[c])

    def sends(c, d, wait):
        for step in (-d, d):
            target = z + step

            @pl.when(jnp.logical_and(target >= 1, target <= chips - 2))
            def _():
                copy = direct(c, z, jnp.clip(target, 0, chips - 1))
                if wait:
                    copy.wait_send()
                else:
                    copy.start()

    def arrive(c, d):
        for step in (-d, d):
            source = z + step

            @pl.when(jnp.logical_and(inner, jnp.logical_and(source >= 0, source <= chips - 1)))
            def _():
                zz = jnp.clip(source, 0, chips - 1)
                direct(c, zz, z).wait_recv()
                cross(c, zz, slot(c, 2 * zz + k)).start()

    def part_copy(g, j):
        to_orb, where = peer(j)
        return remote(parts.at[g, j % reps, pl.ds(to_orb * rows_out, rows_out), :], arrived.at[g, j - 1],
                      part_send.at[g, j - 1], part_recv.at[g, j - 1], where)

    def end_copy(g, j):
        to_orb, where = peer(j)
        return remote(end_parts.at[g, j % reps, pl.ds(to_orb * rows_out, rows_out), :], end_arrived.at[g, j],
                      end_send.at[g, j], end_recv.at[g, j], dict(where, aux=end_aux))

    def self_copy(j):
        to_orb, where = peer(j)
        return remote(self_parts.at[j % reps, pl.ds(to_orb * rows_out, rows_out), :], self_arrived.at[j - 1],
                      self_send.at[j - 1], self_recv.at[j - 1], where)

    def prepare(c):
        raw_copy(c).wait()
        for n in range(rows_piece // chunk):
            first = c * rows_piece + n * chunk
            span = pl.ds(first, chunk)
            turned = pltpu.einshape("ald->lad", raw[span])
            block = first // BLOCK
            weight = jnp.concatenate(
                [jnp.full((chunk, BLOCK), mask_ref[block, b].astype(F32)) for b in range(orb_cols // BLOCK)], 1
            ).astype(BF16)
            for i in range(half):
                mine = turned[i]
                for q in range(1, reps):
                    mine = jnp.where(r == q, turned[q * half + i], mine)
                masked[i, span, :] = mine * weight

    def flat_dot(block, dens):
        count = block.shape[1]
        made = jnp.dot(block.reshape(half * count, orb_cols), dens[...], preferred_element_type=F32).astype(BF16)
        return jnp.concatenate([made[i * count:(i + 1) * count] for i in range(half)], 1)

    def tile(which, block):
        moved = flat_dot(block, virt_dens)
        return lax.dot_general(occ[which], moved, CONTRACT, preferred_element_type=F32) * factor

    prepare(0)
    pl.semaphore_wait(
        barrier,
        peers + jnp.where(inner, chips - 1, chips - 2)
        + jnp.where(jnp.logical_or(feeds, at_end), peers - 1, 0),
    )
    for c in range(pieces):
        if c > 0:
            prepare(c)
        sends(c, 1, False)

        @pl.when(inner)
        def _():
            cross(c, z, piece(c)).start()
            local(c).start()
    for d in range(2, chips - 1):
        for c in range(pieces):
            sends(c, d, False)

    occ_copy.wait()
    virt_copy.wait()
    for c in range(pieces):
        occ[0, rows(c), :] = flat_dot(masked[:, rows(c), :], occ_dens)
    for s in reversed(range(reps)):
        side = (r + s) % reps
        total = tile(0, masked[:, pl.ds(side * self_cols, self_cols), :])
        self_parts[s] = total.astype(BF16)
        if s == 0:
            self_whole[...] = total
        for j in range(1, peers):
            if j % reps == s:
                self_copy(j).start()

    for d in range(1, chips - 2):
        for c in range(pieces):
            arrive(c, d)
            if d == 1:
                @pl.when(feeds)
                def _():
                    rows_e = gath[c // per_group][end_aux, :, pl.ds(c % per_group * rows_piece, rows_piece), :]
                    occ[1, rows(c), :] = flat_dot(rows_e, occ_dens)

    def group(g):
        span = range(g * per_group, (g + 1) * per_group)
        for c in span:
            arrive(c, chips - 2)

        @pl.when(inner)
        def _():
            for c in span:
                for zz in range(chips):
                    cross(c, zz, slot(c, 2 * zz + 1 - k)).wait_recv()
                local(c).wait()

            @pl.when(feeds)
            def _():
                for s in reversed(range(reps)):
                    partner = match_ref[(r + s) % reps, end_aux]
                    end_parts[g, s] = tile(1, gath[g][partner]).astype(BF16)
                    for j in range(peers):
                        if j % reps == s:
                            end_copy(g, j).start()

            for s in reversed(range(reps)):
                partner = match_ref[(r + s) % reps, a]
                total = tile(0, gath[g][partner])
                parts[g, s] = total.astype(BF16)
                if s == 0:
                    whole[g] = total
                for j in range(1, peers):
                    if j % reps == s:
                        part_copy(g, j).start()

    def finish(g):
        @pl.when(inner)
        def _():
            total = whole[g, pl.ds(o * rows_out, rows_out), :]
            for j in range(1, peers):
                part_copy(g, j).wait_recv()
                total = total + arrived[g, j - 1].astype(F32)
            pair_out[:, g * cols_group:(g + 1) * cols_group] = total

    def finish_end(g):
        @pl.when(at_end)
        def _():
            total = None
            for j in range(peers):
                end_copy(g, j).wait_recv()
                term = end_arrived[g, j].astype(F32)
                total = term if total is None else total + term
            pair_out[:, g * cols_group:(g + 1) * cols_group] = total

    def finish_self():
        total = self_whole[pl.ds(o * rows_out, rows_out), :]
        for j in range(1, peers):
            self_copy(j).wait_recv()
            total = total + self_arrived[j - 1].astype(F32)
        self_out[...] = total

    finish_self()
    for g in range(groups):
        group(g)
        if g > 0:
            finish(g - 1)
        finish_end(g)
    finish(groups - 1)

    for c in range(pieces):
        for d in range(1, chips - 1):
            sends(c, d, True)

        @pl.when(inner)
        def _():
            for zz in range(chips):
                cross(c, zz, piece(c)).wait_send()
    for j in range(1, peers):
        self_copy(j).wait_send()
    for g in range(groups):
        @pl.when(inner)
        def _():
            for j in range(1, peers):
                part_copy(g, j).wait_send()

        @pl.when(feeds)
        def _():
            for j in range(peers):
                end_copy(g, j).wait_send()


def per_device(slab, occ_density, virt_density, block_mask, matching):
    owners = lax.axis_size("aux")
    orbs = lax.axis_size("orb")
    reps = lax.axis_size("rep")
    chips = owners // 2
    aux_rows, batch, orb_cols = slab.shape
    pieces = max(2, 32 // chips)
    rows_piece = aux_rows // pieces
    per_group = max(1, BLOCK // rows_piece)
    groups = pieces // per_group
    cols_group = per_group * rows_piece
    half = batch // reps
    rows_out = aux_rows // orbs
    self_cols = aux_rows // reps
    peers = orbs * reps
    chunk = min(rows_piece, BLOCK // 2)
    factor = 1.0 / math.sqrt(batch * orb_cols * orbs)
    dma = pltpu.SemaphoreType.DMA
    vmem = pl.BlockSpec(memory_space=pltpu.VMEM)
    smem = pl.BlockSpec(memory_space=pltpu.SMEM)
    hbm = pl.BlockSpec(memory_space=pltpu.HBM)
    buffers = [((owners, half, cols_group, orb_cols), BF16) for _ in range(groups)] + [
        ((aux_rows, batch, orb_cols), BF16),
        ((half, aux_rows, orb_cols), BF16),
        ((orb_cols, orb_cols), BF16),
        ((orb_cols, orb_cols), BF16),
        ((2, aux_rows, half * orb_cols), BF16),
        ((groups, reps, aux_rows, cols_group), BF16),
        ((groups, reps, aux_rows, cols_group), BF16),
        ((groups, aux_rows, cols_group), F32),
        ((groups, peers - 1, rows_out, cols_group), BF16),
        ((groups, peers, rows_out, cols_group), BF16),
        ((reps, aux_rows, self_cols), BF16),
        ((aux_rows, self_cols), F32),
        ((peers - 1, rows_out, self_cols), BF16),
    ]
    held = sum(math.prod(shape) * jnp.dtype(kind).itemsize for shape, kind in buffers)
    pair, own = pl.pallas_call(
        functools.partial(kernel, (chips, orbs, reps, pieces, groups, chunk), factor),
        out_shape=(
            jax.ShapeDtypeStruct((rows_out, aux_rows), F32),
            jax.ShapeDtypeStruct((rows_out, self_cols), F32),
        ),
        in_specs=[smem, smem, hbm, hbm, hbm],
        out_specs=(vmem, vmem),
        scratch_shapes=[pltpu.VMEM(shape, kind) for shape, kind in buffers] + [
            dma((pieces,)), dma((2,)), dma((pieces,)),
            dma((pieces, chips)), dma((pieces, chips)), dma((pieces, chips)), dma((pieces, chips)),
            dma((groups, peers - 1)), dma((groups, peers - 1)),
            dma((groups, peers)), dma((groups, peers)),
            dma((peers - 1,)), dma((peers - 1,)),
        ],
        compiler_params=pltpu.CompilerParams(
            collective_id=0, has_side_effects=True, vmem_limit_bytes=held + 8 * 2**20
        ),
    )(matching, block_mask, slab, occ_density, virt_density)
    return (pair[None], own)


def solution(mesh):
    return jax.shard_map(
        per_device,
        mesh=mesh,
        in_specs=(P("aux", None, "orb"), P("orb", None), P("orb", None), P("aux", "orb"), P()),
        out_specs=(P("rep", ("aux", "orb"), None), P(("aux", "orb"), "rep")),
        check_vma=False,
    )
```

time: 79.2 us -> 85.4 us (1.078)
  the two profiles are of different devices: /device:TPU:1 before, /device:TPU:24 now
where the time goes in v1:
time: 85.4 us; the launch traced here: 85.1 us
  Pallas kernels  77.9 us (91%)
  local copies, waits for them, and re-layouts  6.52 us (8%)
    pallas_call x1, Pallas kernels, per_device(): pl.pallas_call(functools.partial(kernel, (chips, orbs, reps, pieces, grou...  77.9 us
    unnamed x12, local copies, waits for them, and re-layouts  6.52 us

profile of v1, /device:TPU:24, one launch (start us, length us, event | category | flops | bytes accessed | tf_op | source)
XLA Modules:
  0.0 85.1 jit_solution(6781792179304837461)
XLA Ops:
  0.6 0.0 copy-start
  0.6 1.6 %copy-done = bf16[512,4,512]{2,1,0:T(4,128)(2,1)S(1)} copy-done((bf16[512,4,512]{2,1,0:T(4,128)(2,1)S(1)}, bf16[512,4,512]{2,1,0:T(4,128)(2,1)}, u32[]{:S(2)}) %copy-start) | copy-done | bytes 2097176
  2.2 0.0 copy-start.1
  2.2 1.0 %copy-done.1 = bf16[512,512]{1,0:T(8,128)(2,1)S(1)} copy-done((bf16[512,512]{1,0:T(8,128)(2,1)S(1)}, bf16[512,512]{1,0:T(8,128)(2,1)}, u32[]{:S(2)}) %copy-start.1) | copy-done | bytes 524312
  3.3 0.0 copy-start.2
  3.3 1.0 %copy-done.2 = bf16[512,512]{1,0:T(8,128)(2,1)S(1)} copy-done((bf16[512,512]{1,0:T(8,128)(2,1)S(1)}, bf16[512,512]{1,0:T(8,128)(2,1)}, u32[]{:S(2)}) %copy-start.2) | copy-done | bytes 524312
  4.3 0.0 copy-start.3
  4.3 0.7 copy-done.3
  5.0 0.0 copy-start.4
  5.0 0.7 copy-done.4
  5.7 77.9 %shard_map.68 = (f32[256,512]{1,0:T(8,128)S(1)}, f32[256,256]{1,0:T(8,128)S(1)}) custom-call(s32[2,8]{1,0:T(2,128)S(1)} %copy-done.4, s32[4,4]{1,0:T(4,128)S(1)} %copy-done.3, bf16[512,4,512]{2,1,0:T(4,128)(2,1)S(1)} %copy-done, bf16[512,512]{1,0:T(8,128)(2,1)S(1)} %copy-done.1, bf16[512,512]{1,0:T(8,128)(2,1)S(1)} %copy-done.2), custom_call_target="tpu_custom_call" | custom-call | tf_op jit(solution)/shard_map/pallas_call | solution.py:335
  83.6 0.8 copy.9
  84.4 0.7 copy.10
Async XLA Ops:
  0.6 1.6 %copy-start = (bf16[512,4,512]{2,1,0:T(4,128)(2,1)S(1)}, bf16[512,4,512]{2,1,0:T(4,128)(2,1)}, u32[]{:S(2)}) copy-start(bf16[512,4,512]{2,1,0:T(4,128)(2,1)} %slab.1) | copy-start | bytes 6291460
  2.2 1.0 %copy-start.1 = (bf16[512,512]{1,0:T(8,128)(2,1)S(1)}, bf16[512,512]{1,0:T(8,128)(2,1)}, u32[]{:S(2)}) copy-start(bf16[512,512]{1,0:T(8,128)(2,1)} %occ_hbm.1) | copy-start | bytes 1572868
  3.3 1.0 %copy-start.2 = (bf16[512,512]{1,0:T(8,128)(2,1)S(1)}, bf16[512,512]{1,0:T(8,128)(2,1)}, u32[]{:S(2)}) copy-start(bf16[512,512]{1,0:T(8,128)(2,1)} %virt_hbm.1) | copy-start | bytes 1572868
  4.3 0.7 copy-start.3
  5.0 0.7 copy-start.4

commit v2 on v1

--- a/solution.py
+++ b/solution.py
@@ -14,12 +14,12 @@
 F32, BF16 = jnp.float32, jnp.bfloat16
 
 
-def kernel(sizes, factor, match_ref, mask_ref, slab, occ_hbm, virt_hbm, pair_out, self_out, *scratch):
+def kernel(sizes, factor, match_hbm, mask_hbm, slab, occ_hbm, virt_hbm, pair_out, self_out, *scratch):
     chips, orbs, reps, pieces, groups, chunk = sizes
     gath = scratch[:groups]
-    (raw, masked, occ_dens, virt_dens, occ, parts, end_parts, whole, arrived, end_arrived,
-     self_parts, self_whole, self_arrived, raw_sem, dens_sem, local_sem, send_sem, recv_sem,
-     core_send, core_recv, part_send, part_recv, end_send, end_recv, self_send, self_recv) = scratch[groups:]
+    (match_ref, mask_ref, raw, masked, occ_dens, virt_dens, occ, parts, end_parts, whole, arrived, end_arrived,
+     self_parts, self_whole, self_arrived, small_sem, raw_sem, dens_sem, local_sem, up_sem, down_sem,
+     recv_sem, core_send, core_recv, part_send, part_recv, end_send, end_recv, self_send, self_recv) = scratch[groups:]
     half, aux_rows, orb_cols = masked.shape
     rows_piece = aux_rows // pieces
     per_group = pieces // groups
@@ -39,6 +39,8 @@
     end_aux = jnp.where(z == 1, k, 2 * (chips - 1) + k)
     feed_aux = jnp.where(z == 0, 2 + k, 2 * (chips - 2) + k)
     other = 2 * z + 1 - k
+    up_ok = z + 1 <= chips - 2
+    down_ok = z - 1 >= 1
 
     def peer(j):
         to_orb, to_rep = (o + j // reps) % orbs, (r + j % reps) % reps
@@ -50,8 +52,12 @@
     def raw_copy(c):
         return pltpu.make_async_copy(slab.at[rows(c)], raw.at[rows(c)], raw_sem.at[c])
 
+    mask_copy = pltpu.make_async_copy(mask_hbm, mask_ref, small_sem.at[0])
+    match_copy = pltpu.make_async_copy(match_hbm, match_ref, small_sem.at[1])
+    mask_copy.start()
     for c in range(pieces):
         raw_copy(c).start()
+    match_copy.start()
     occ_copy = pltpu.make_async_copy(occ_hbm, occ_dens, dens_sem.at[0])
     virt_copy = pltpu.make_async_copy(virt_hbm, virt_dens, dens_sem.at[1])
     occ_copy.start()
@@ -62,14 +68,13 @@
     def greet(where):
         pl.semaphore_signal(barrier, inc=1, device_id=where, device_id_type=MESH)
 
-    for d in range(1, chips):
-        @pl.when(jnp.logical_and(z - d >= 0, jnp.logical_or(inner, z - d >= 1)))
-        def _():
-            greet({"aux": a - 2 * d})
-
-        @pl.when(jnp.logical_and(z + d <= chips - 1, jnp.logical_or(inner, z + d <= chips - 2)))
-        def _():
-            greet({"aux": a + 2 * d})
+    @pl.when(z > 0)
+    def _():
+        greet({"aux": a - 2})
+
+    @pl.when(z < chips - 1)
+    def _():
+        greet({"aux": a + 2})
 
     greet({"aux": other})
     for j in range(1, peers):
@@ -94,9 +99,11 @@
     def slot(c, owner):
         return gath[c // per_group].at[owner, :, pl.ds(c % per_group * rows_piece, rows_piece), :]
 
-    def direct(c, source, target):
-        return remote(piece(c), slot(c, 2 * source + k), send_sem.at[c, target], recv_sem.at[c, source],
-                      {"aux": 2 * target + k})
+    def up(c, zz, src):
+        return remote(src, slot(c, 2 * zz + k), up_sem.at[c, zz], recv_sem.at[c, zz], {"aux": a + 2})
+
+    def down(c, zz, src):
+        return remote(src, slot(c, 2 * zz + k), down_sem.at[c, zz], recv_sem.at[c, zz], {"aux": a - 2})
 
     def cross(c, zz, src):
         return remote(src, slot(c, 2 * zz + k), core_send.at[c, zz], core_recv.at[c, zz], {"aux": other})
@@ -104,27 +111,59 @@
     def local(c):
         return pltpu.make_async_copy(piece(c), slot(c, a), local_sem.at[c])
 
-    def sends(c, d, wait):
-        for step in (-d, d):
-            target = z + step
-
-            @pl.when(jnp.logical_and(target >= 1, target <= chips - 2))
-            def _():
-                copy = direct(c, z, jnp.clip(target, 0, chips - 1))
-                if wait:
-                    copy.wait_send()
-                else:
-                    copy.start()
-
-    def arrive(c, d):
-        for step in (-d, d):
-            source = z + step
-
-            @pl.when(jnp.logical_and(inner, jnp.logical_and(source >= 0, source <= chips - 1)))
-            def _():
-                zz = jnp.clip(source, 0, chips - 1)
-                direct(c, zz, z).wait_recv()
+    def lower(c, send):
+        for d in range(1, chips):
+            @pl.when(z - d >= 0)
+            def _():
+                zz = jnp.maximum(z - d, 0)
+                up(c, zz, slot(c, 2 * zz + k)).wait_recv()
+                if send:
+                    up(c, zz, slot(c, 2 * zz + k)).start()
                 cross(c, zz, slot(c, 2 * zz + k)).start()
+
+    def upper(c, send):
+        for d in range(1, chips):
+            @pl.when(z + d <= chips - 1)
+            def _():
+                zz = jnp.minimum(z + d, chips - 1)
+                down(c, zz, slot(c, 2 * zz + k)).wait_recv()
+                if send:
+                    down(c, zz, slot(c, 2 * zz + k)).start()
+                cross(c, zz, slot(c, 2 * zz + k)).start()
+
+    def own(c):
+        @pl.when(up_ok)
+        def _():
+            up(c, z, piece(c)).start()
+
+        @pl.when(down_ok)
+        def _():
+            down(c, z, piece(c)).start()
+
+    def relay(c):
+        @pl.when(jnp.logical_and(inner, up_ok))
+        def _():
+            lower(c, True)
+
+        @pl.when(jnp.logical_and(inner, down_ok))
+        def _():
+            upper(c, True)
+
+        @pl.when(feeds)
+        def _():
+            rows_e = gath[c // per_group][end_aux, :, pl.ds(c % per_group * rows_piece, rows_piece), :]
+            occ[1, rows(c), :] = flat_dot(rows_e, occ_dens)
+
+    def complete(c):
+        @pl.when(inner)
+        def _():
+            @pl.when(jnp.logical_not(up_ok))
+            def _():
+                lower(c, False)
+
+            @pl.when(jnp.logical_not(down_ok))
+            def _():
+                upper(c, False)
 
     def part_copy(g, j):
         to_orb, where = peer(j)
@@ -166,69 +205,27 @@
         moved = flat_dot(block, virt_dens)
         return lax.dot_general(occ[which], moved, CONTRACT, preferred_element_type=F32) * factor
 
-    prepare(0)
-    pl.semaphore_wait(
-        barrier,
-        peers + jnp.where(inner, chips - 1, chips - 2)
-        + jnp.where(jnp.logical_or(feeds, at_end), peers - 1, 0),
-    )
-    for c in range(pieces):
-        if c > 0:
-            prepare(c)
-        sends(c, 1, False)
-
-        @pl.when(inner)
-        def _():
-            cross(c, z, piece(c)).start()
-            local(c).start()
-    for d in range(2, chips - 1):
-        for c in range(pieces):
-            sends(c, d, False)
-
-    occ_copy.wait()
-    virt_copy.wait()
-    for c in range(pieces):
-        occ[0, rows(c), :] = flat_dot(masked[:, rows(c), :], occ_dens)
-    for s in reversed(range(reps)):
-        side = (r + s) % reps
-        total = tile(0, masked[:, pl.ds(side * self_cols, self_cols), :])
-        self_parts[s] = total.astype(BF16)
-        if s == 0:
-            self_whole[...] = total
-        for j in range(1, peers):
-            if j % reps == s:
-                self_copy(j).start()
-
-    for d in range(1, chips - 2):
-        for c in range(pieces):
-            arrive(c, d)
-            if d == 1:
-                @pl.when(feeds)
-                def _():
-                    rows_e = gath[c // per_group][end_aux, :, pl.ds(c % per_group * rows_piece, rows_piece), :]
-                    occ[1, rows(c), :] = flat_dot(rows_e, occ_dens)
-
-    def group(g):
-        span = range(g * per_group, (g + 1) * per_group)
-        for c in span:
-            arrive(c, chips - 2)
-
-        @pl.when(inner)
-        def _():
-            for c in span:
+    def gathered(g):
+        @pl.when(inner)
+        def _():
+            for c in range(g * per_group, (g + 1) * per_group):
                 for zz in range(chips):
                     cross(c, zz, slot(c, 2 * zz + 1 - k)).wait_recv()
                 local(c).wait()
 
-            @pl.when(feeds)
-            def _():
-                for s in reversed(range(reps)):
-                    partner = match_ref[(r + s) % reps, end_aux]
-                    end_parts[g, s] = tile(1, gath[g][partner]).astype(BF16)
-                    for j in range(peers):
-                        if j % reps == s:
-                            end_copy(g, j).start()
-
+    def end_tiles(g):
+        @pl.when(feeds)
+        def _():
+            for s in reversed(range(reps)):
+                partner = match_ref[(r + s) % reps, end_aux]
+                end_parts[g, s] = tile(1, gath[g][partner]).astype(BF16)
+                for j in range(peers):
+                    if j % reps == s:
+                        end_copy(g, j).start()
+
+    def own_tiles(g):
+        @pl.when(inner)
+        def _():
             for s in reversed(range(reps)):
                 partner = match_ref[(r + s) % reps, a]
                 total = tile(0, gath[g][partner])
@@ -239,6 +236,17 @@
                     if j % reps == s:
                         part_copy(g, j).start()
 
+    def self_tiles():
+        for s in reversed(range(reps)):
+            side = (r + s) % reps
+            total = tile(0, masked[:, pl.ds(side * self_cols, self_cols), :])
+            self_parts[s] = total.astype(BF16)
+            if s == 0:
+                self_whole[...] = total
+            for j in range(1, peers):
+                if j % reps == s:
+                    self_copy(j).start()
+
     def finish(g):
         @pl.when(inner)
         def _():
@@ -265,17 +273,64 @@
             total = total + self_arrived[j - 1].astype(F32)
         self_out[...] = total
 
-    finish_self()
+    mask_copy.wait()
+    for c in range(pieces):
+        prepare(c)
+        if c == 0:
+            pl.semaphore_wait(
+                barrier,
+                peers + jnp.where(inner, 2, 1) + jnp.where(jnp.logical_or(feeds, at_end), peers - 1, 0),
+            )
+        if c < 2:
+            own(c)
+
+        @pl.when(inner)
+        def _():
+            cross(c, z, piece(c)).start()
+            local(c).start()
+
+    match_copy.wait()
+    occ_copy.wait()
+    virt_copy.wait()
+    for c in range(pieces):
+        occ[0, rows(c), :] = flat_dot(masked[:, rows(c), :], occ_dens)
+    ahead = min(3, pieces)
+    for c in range(ahead):
+        relay(c)
+        if c == 0:
+            self_tiles()
+    made = ended = closed = 0
+    for c in range(pieces):
+        if c + 2 < pieces:
+            own(c + 2)
+        if c + ahead < pieces:
+            relay(c + ahead)
+        complete(c)
+        if (c + 1) % per_group == 0:
+            g = c // per_group
+            gathered(g)
+            if c + ahead >= pieces - 1:
+                for e in range(ended, g + 1):
+                    end_tiles(e)
+                ended = g + 1
+            own_tiles(g)
+            if g == 0:
+                finish_self()
+            else:
+                finish(g - 1)
+    finish(groups - 1)
     for g in range(groups):
-        group(g)
-        if g > 0:
-            finish(g - 1)
         finish_end(g)
-    finish(groups - 1)
 
     for c in range(pieces):
-        for d in range(1, chips - 1):
-            sends(c, d, True)
+        for d in range(chips):
+            @pl.when(jnp.logical_and(up_ok, z - d >= 0))
+            def _():
+                up(c, jnp.maximum(z - d, 0), piece(c)).wait_send()
+
+            @pl.when(jnp.logical_and(down_ok, z + d <= chips - 1))
+            def _():
+                down(c, jnp.minimum(z + d, chips - 1), piece(c)).wait_send()
 
         @pl.when(inner)
         def _():
@@ -314,9 +369,9 @@
     factor = 1.0 / math.sqrt(batch * orb_cols * orbs)
     dma = pltpu.SemaphoreType.DMA
     vmem = pl.BlockSpec(memory_space=pltpu.VMEM)
-    smem = pl.BlockSpec(memory_space=pltpu.SMEM)
     hbm = pl.BlockSpec(memory_space=pltpu.HBM)
-    buffers = [((owners, half, cols_group, orb_cols), BF16) for _ in range(groups)] + [
+    gathers = [pltpu.VMEM((owners, half, cols_group, orb_cols), BF16) for _ in range(groups)]
+    buffers = [
         ((aux_rows, batch, orb_cols), BF16),
         ((half, aux_rows, orb_cols), BF16),
         ((orb_cols, orb_cols), BF16),
@@ -332,16 +387,19 @@
         ((peers - 1, rows_out, self_cols), BF16),
     ]
     held = sum(math.prod(shape) * jnp.dtype(kind).itemsize for shape, kind in buffers)
+    held += owners * half * aux_rows * orb_cols * jnp.dtype(BF16).itemsize
     pair, own = pl.pallas_call(
         functools.partial(kernel, (chips, orbs, reps, pieces, groups, chunk), factor),
         out_shape=(
             jax.ShapeDtypeStruct((rows_out, aux_rows), F32),
             jax.ShapeDtypeStruct((rows_out, self_cols), F32),
         ),
-        in_specs=[smem, smem, hbm, hbm, hbm],
+        in_specs=[hbm] * 5,
         out_specs=(vmem, vmem),
-        scratch_shapes=[pltpu.VMEM(shape, kind) for shape, kind in buffers] + [
-            dma((pieces,)), dma((2,)), dma((pieces,)),
+        scratch_shapes=gathers + [
+            pltpu.SMEM(matching.shape, matching.dtype), pltpu.SMEM(block_mask.shape, block_mask.dtype),
+        ] + [pltpu.VMEM(shape, kind) for shape, kind in buffers] + [
+            dma((2,)), dma((pieces,)), dma((2,)), dma((pieces,)), dma((pieces, chips)),
             dma((pieces, chips)), dma((pieces, chips)), dma((pieces, chips)), dma((pieces, chips)),
             dma((groups, peers - 1)), dma((groups, peers - 1)),
             dma((groups, peers)), dma((groups, peers)),
@@ -350,7 +408,8 @@
         compiler_params=pltpu.CompilerParams(
             collective_id=0, has_side_effects=True, vmem_limit_bytes=held + 8 * 2**20
         ),
-    )(matching, block_mask, slab, occ_density, virt_density)
+    )(*(pltpu.with_memory_space_constraint(x, pltpu.HBM)
+        for x in (matching, block_mask, slab, occ_density, virt_density)))
     return (pair[None], own)
 
 

time: 85.4 us -> 72.3 us (0.85)
  the two profiles are of different devices: /device:TPU:24 before, /device:TPU:1 now
where the time goes in v2:
time: 72.3 us; the launch traced here: 72.2 us
  Pallas kernels  70 us (97%)
  local copies, waits for them, and re-layouts  1.5 us (2%)
    pallas_call x1, Pallas kernels, per_device(): pl.pallas_call(functools.partial(kernel, (chips, orbs, reps, pieces, grou...  70 us
    unnamed x2, local copies, waits for them, and re-layouts  1.5 us

profile of v2, /device:TPU:1, one launch (start us, length us, event | category | flops | bytes accessed | tf_op | source)
XLA Modules:
  0.0 72.2 jit_solution(1656031035440663894)
XLA Ops:
  0.6 70.0 %shard_map.68 = (f32[256,512]{1,0:T(8,128)S(1)}, f32[256,256]{1,0:T(8,128)S(1)}) custom-call(s32[2,8]{1,0:T(2,128)} %match_hbm.1, s32[4,4]{1,0:T(4,128)} %mask_hbm.1, bf16[512,4,512]{2,1,0:T(4,128)(2,1)} %slab.1, bf16[512,512]{1,0:T(8,128)(2,1)} %occ_hbm.1, bf16[512,512]{1,0:T(8,128)(2,1)} %virt_hbm.1), custom_call_target="tpu_custom_call" | custom-call | tf_op jit(solution)/shard_map/pallas_call | solution.py:391
  70.7 0.8 %copy.9 = f32[1,256,512]{2,1,0:T(8,128)} copy(f32[1,256,512]{2,1,0:T(8,128)S(1)} %bitcast.1) | data formatting | bytes 1048576
  71.5 0.7 copy.10

commit v3 on v2

--- a/solution.py
+++ b/solution.py
@@ -15,15 +15,13 @@
 
 
 def kernel(sizes, factor, match_hbm, mask_hbm, slab, occ_hbm, virt_hbm, pair_out, self_out, *scratch):
-    chips, orbs, reps, pieces, groups, chunk = sizes
-    gath = scratch[:groups]
+    chips, orbs, reps, pieces, chunk = sizes
+    gath = scratch[:pieces]
     (match_ref, mask_ref, raw, masked, occ_dens, virt_dens, occ, parts, end_parts, whole, arrived, end_arrived,
      self_parts, self_whole, self_arrived, small_sem, raw_sem, dens_sem, local_sem, up_sem, down_sem,
-     recv_sem, core_send, core_recv, part_send, part_recv, end_send, end_recv, self_send, self_recv) = scratch[groups:]
+     recv_sem, core_send, core_recv, part_send, part_recv, end_send, end_recv, self_send, self_recv) = scratch[pieces:]
     half, aux_rows, orb_cols = masked.shape
     rows_piece = aux_rows // pieces
-    per_group = pieces // groups
-    cols_group = aux_rows // groups
     rows_out = aux_rows // orbs
     self_cols = aux_rows // reps
     peers = orbs * reps
@@ -97,7 +95,7 @@
         return masked.at[:, rows(c), :]
 
     def slot(c, owner):
-        return gath[c // per_group].at[owner, :, pl.ds(c % per_group * rows_piece, rows_piece), :]
+        return gath[c].at[owner]
 
     def up(c, zz, src):
         return remote(src, slot(c, 2 * zz + k), up_sem.at[c, zz], recv_sem.at[c, zz], {"aux": a + 2})
@@ -151,8 +149,7 @@
 
         @pl.when(feeds)
         def _():
-            rows_e = gath[c // per_group][end_aux, :, pl.ds(c % per_group * rows_piece, rows_piece), :]
-            occ[1, rows(c), :] = flat_dot(rows_e, occ_dens)
+            occ[1, rows(c), :] = flat_dot(gath[c][end_aux], occ_dens)
 
     def complete(c):
         @pl.when(inner)
@@ -165,15 +162,15 @@
             def _():
                 upper(c, False)
 
-    def part_copy(g, j):
+    def part_copy(c, j):
         to_orb, where = peer(j)
-        return remote(parts.at[g, j % reps, pl.ds(to_orb * rows_out, rows_out), :], arrived.at[g, j - 1],
-                      part_send.at[g, j - 1], part_recv.at[g, j - 1], where)
-
-    def end_copy(g, j):
+        return remote(parts.at[c, j % reps, to_orb], arrived.at[c, j - 1],
+                      part_send.at[c, j - 1], part_recv.at[c, j - 1], where)
+
+    def end_copy(c, j):
         to_orb, where = peer(j)
-        return remote(end_parts.at[g, j % reps, pl.ds(to_orb * rows_out, rows_out), :], end_arrived.at[g, j],
-                      end_send.at[g, j], end_recv.at[g, j], dict(where, aux=end_aux))
+        return remote(end_parts.at[c, j % reps, to_orb], end_arrived.at[c, j],
+                      end_send.at[c, j], end_recv.at[c, j], dict(where, aux=end_aux))
 
     def self_copy(j):
         to_orb, where = peer(j)
@@ -201,45 +198,50 @@
         made = jnp.dot(block.reshape(half * count, orb_cols), dens[...], preferred_element_type=F32).astype(BF16)
         return jnp.concatenate([made[i * count:(i + 1) * count] for i in range(half)], 1)
 
-    def tile(which, block):
+    def self_tile(block):
         moved = flat_dot(block, virt_dens)
-        return lax.dot_general(occ[which], moved, CONTRACT, preferred_element_type=F32) * factor
-
-    def gathered(g):
-        @pl.when(inner)
-        def _():
-            for c in range(g * per_group, (g + 1) * per_group):
-                for zz in range(chips):
-                    cross(c, zz, slot(c, 2 * zz + 1 - k)).wait_recv()
-                local(c).wait()
-
-    def end_tiles(g):
+        return lax.dot_general(occ[0], moved, CONTRACT, preferred_element_type=F32) * factor
+
+    def turned_tiles(c, which, owner):
+        blocks = jnp.concatenate([gath[c][match_ref[(r + s) % reps, owner]] for s in range(reps)], 1)
+        moved = flat_dot(blocks, virt_dens)
+        total = lax.dot_general(moved, occ[which], CONTRACT, preferred_element_type=F32) * factor
+        return [[total[s * rows_piece:(s + 1) * rows_piece, q * rows_out:(q + 1) * rows_out]
+                 for q in range(orbs)] for s in range(reps)]
+
+    def gathered(c):
+        @pl.when(inner)
+        def _():
+            for zz in range(chips):
+                cross(c, zz, slot(c, 2 * zz + 1 - k)).wait_recv()
+            local(c).wait()
+
+    def end_tiles(c):
         @pl.when(feeds)
         def _():
+            tiles = turned_tiles(c, 1, end_aux)
             for s in reversed(range(reps)):
-                partner = match_ref[(r + s) % reps, end_aux]
-                end_parts[g, s] = tile(1, gath[g][partner]).astype(BF16)
-                for j in range(peers):
-                    if j % reps == s:
-                        end_copy(g, j).start()
-
-    def own_tiles(g):
-        @pl.when(inner)
-        def _():
+                for q in range(orbs):
+                    end_parts[c, s, q] = tiles[s][q].astype(BF16)
+            for j in reversed(range(peers)):
+                end_copy(c, j).start()
+
+    def own_tiles(c):
+        @pl.when(inner)
+        def _():
+            tiles = turned_tiles(c, 0, a)
             for s in reversed(range(reps)):
-                partner = match_ref[(r + s) % reps, a]
-                total = tile(0, gath[g][partner])
-                parts[g, s] = total.astype(BF16)
-                if s == 0:
-                    whole[g] = total
-                for j in range(1, peers):
-                    if j % reps == s:
-                        part_copy(g, j).start()
+                for q in range(orbs):
+                    parts[c, s, q] = tiles[s][q].astype(BF16)
+                    if s == 0:
+                        whole[c, q] = tiles[s][q]
+            for j in reversed(range(1, peers)):
+                part_copy(c, j).start()
 
     def self_tiles():
         for s in reversed(range(reps)):
             side = (r + s) % reps
-            total = tile(0, masked[:, pl.ds(side * self_cols, self_cols), :])
+            total = self_tile(masked[:, pl.ds(side * self_cols, self_cols), :])
             self_parts[s] = total.astype(BF16)
             if s == 0:
                 self_whole[...] = total
@@ -247,24 +249,27 @@
                 if j % reps == s:
                     self_copy(j).start()
 
-    def finish(g):
-        @pl.when(inner)
-        def _():
-            total = whole[g, pl.ds(o * rows_out, rows_out), :]
+    def columns(c):
+        return slice(c * rows_piece, (c + 1) * rows_piece)
+
+    def finish(c):
+        @pl.when(inner)
+        def _():
+            total = whole[c, o]
             for j in range(1, peers):
-                part_copy(g, j).wait_recv()
-                total = total + arrived[g, j - 1].astype(F32)
-            pair_out[:, g * cols_group:(g + 1) * cols_group] = total
-
-    def finish_end(g):
+                part_copy(c, j).wait_recv()
+                total = total + arrived[c, j - 1].astype(F32)
+            pair_out[:, columns(c)] = total.T
+
+    def finish_end(c):
         @pl.when(at_end)
         def _():
             total = None
             for j in range(peers):
-                end_copy(g, j).wait_recv()
-                term = end_arrived[g, j].astype(F32)
+                end_copy(c, j).wait_recv()
+                term = end_arrived[c, j].astype(F32)
                 total = term if total is None else total + term
-            pair_out[:, g * cols_group:(g + 1) * cols_group] = total
+            pair_out[:, columns(c)] = total.T
 
     def finish_self():
         total = self_whole[pl.ds(o * rows_out, rows_out), :]
@@ -299,28 +304,31 @@
         relay(c)
         if c == 0:
             self_tiles()
-    made = ended = closed = 0
+    ended = 0
+    lag = 2
     for c in range(pieces):
         if c + 2 < pieces:
             own(c + 2)
         if c + ahead < pieces:
             relay(c + ahead)
+        filled = c + ahead >= pieces - 1
+        while filled and ended < c:
+            end_tiles(ended)
+            ended += 1
         complete(c)
-        if (c + 1) % per_group == 0:
-            g = c // per_group
-            gathered(g)
-            if c + ahead >= pieces - 1:
-                for e in range(ended, g + 1):
-                    end_tiles(e)
-                ended = g + 1
-            own_tiles(g)
-            if g == 0:
-                finish_self()
-            else:
-                finish(g - 1)
-    finish(groups - 1)
-    for g in range(groups):
-        finish_end(g)
+        gathered(c)
+        if filled:
+            end_tiles(c)
+            ended += 1
+        own_tiles(c)
+        if c == 0:
+            finish_self()
+        if c >= lag:
+            finish(c - lag)
+    for c in range(max(0, pieces - lag), pieces):
+        finish(c)
+    for c in range(pieces):
+        finish_end(c)
 
     for c in range(pieces):
         for d in range(chips):
@@ -338,16 +346,16 @@
                 cross(c, zz, piece(c)).wait_send()
     for j in range(1, peers):
         self_copy(j).wait_send()
-    for g in range(groups):
+    for c in range(pieces):
         @pl.when(inner)
         def _():
             for j in range(1, peers):
-                part_copy(g, j).wait_send()
+                part_copy(c, j).wait_send()
 
         @pl.when(feeds)
         def _():
             for j in range(peers):
-                end_copy(g, j).wait_send()
+                end_copy(c, j).wait_send()
 
 
 def per_device(slab, occ_density, virt_density, block_mask, matching):
@@ -358,9 +366,6 @@
     aux_rows, batch, orb_cols = slab.shape
     pieces = max(2, 32 // chips)
     rows_piece = aux_rows // pieces
-    per_group = max(1, BLOCK // rows_piece)
-    groups = pieces // per_group
-    cols_group = per_group * rows_piece
     half = batch // reps
     rows_out = aux_rows // orbs
     self_cols = aux_rows // reps
@@ -370,18 +375,18 @@
     dma = pltpu.SemaphoreType.DMA
     vmem = pl.BlockSpec(memory_space=pltpu.VMEM)
     hbm = pl.BlockSpec(memory_space=pltpu.HBM)
-    gathers = [pltpu.VMEM((owners, half, cols_group, orb_cols), BF16) for _ in range(groups)]
+    gathers = [pltpu.VMEM((owners, half, rows_piece, orb_cols), BF16) for _ in range(pieces)]
     buffers = [
         ((aux_rows, batch, orb_cols), BF16),
         ((half, aux_rows, orb_cols), BF16),
         ((orb_cols, orb_cols), BF16),
         ((orb_cols, orb_cols), BF16),
         ((2, aux_rows, half * orb_cols), BF16),
-        ((groups, reps, aux_rows, cols_group), BF16),
-        ((groups, reps, aux_rows, cols_group), BF16),
-        ((groups, aux_rows, cols_group), F32),
-        ((groups, peers - 1, rows_out, cols_group), BF16),
-        ((groups, peers, rows_out, cols_group), BF16),
+        ((pieces, reps, orbs, rows_piece, rows_out), BF16),
+        ((pieces, reps, orbs, rows_piece, rows_out), BF16),
+        ((pieces, orbs, rows_piece, rows_out), F32),
+        ((pieces, peers - 1, rows_piece, rows_out), BF16),
+        ((pieces, peers, rows_piece, rows_out), BF16),
         ((reps, aux_rows, self_cols), BF16),
         ((aux_rows, self_cols), F32),
         ((peers - 1, rows_out, self_cols), BF16),
@@ -389,7 +394,7 @@
     held = sum(math.prod(shape) * jnp.dtype(kind).itemsize for shape, kind in buffers)
     held += owners * half * aux_rows * orb_cols * jnp.dtype(BF16).itemsize
     pair, own = pl.pallas_call(
-        functools.partial(kernel, (chips, orbs, reps, pieces, groups, chunk), factor),
+        functools.partial(kernel, (chips, orbs, reps, pieces, chunk), factor),
         out_shape=(
             jax.ShapeDtypeStruct((rows_out, aux_rows), F32),
             jax.ShapeDtypeStruct((rows_out, self_cols), F32),
@@ -401,8 +406,8 @@
         ] + [pltpu.VMEM(shape, kind) for shape, kind in buffers] + [
             dma((2,)), dma((pieces,)), dma((2,)), dma((pieces,)), dma((pieces, chips)),
             dma((pieces, chips)), dma((pieces, chips)), dma((pieces, chips)), dma((pieces, chips)),
-            dma((groups, peers - 1)), dma((groups, peers - 1)),
-            dma((groups, peers)), dma((groups, peers)),
+            dma((pieces, peers - 1)), dma((pieces, peers - 1)),
+            dma((pieces, peers)), dma((pieces, peers)),
             dma((peers - 1,)), dma((peers - 1,)),
         ],
         compiler_params=pltpu.CompilerParams(

time: 72.3 us -> 63.2 us (0.87)
  Pallas kernels: 70 us -> 60.9 us
    pallas_call x1, Pallas kernels: 70 us -> 60.9 us  [per_device(): pl.pallas_call(functools.partial(kernel, (chips, orbs, reps, pieces, chun...]
where the time goes in v3:
time: 63.2 us; the launch traced here: 63.1 us
  Pallas kernels  60.9 us (96%)
  local copies, waits for them, and re-layouts  1.5 us (2%)
  between operations  0.64 us (1%)
    pallas_call x1, Pallas kernels, per_device(): pl.pallas_call(functools.partial(kernel, (chips, orbs, reps, pieces, chun...  60.9 us
    unnamed x2, local copies, waits for them, and re-layouts  1.5 us

profile of v3, /device:TPU:1, one launch (start us, length us, event | category | flops | bytes accessed | tf_op | source)
XLA Modules:
  0.0 63.1 jit_solution(2546336901304468050)
XLA Ops:
  0.6 60.9 %shard_map.68 = (f32[256,512]{1,0:T(8,128)S(1)}, f32[256,256]{1,0:T(8,128)S(1)}) custom-call(s32[2,8]{1,0:T(2,128)} %match_hbm.1, s32[4,4]{1,0:T(4,128)} %mask_hbm.1, bf16[512,4,512]{2,1,0:T(4,128)(2,1)} %slab.1, bf16[512,512]{1,0:T(8,128)(2,1)} %occ_hbm.1, bf16[512,512]{1,0:T(8,128)(2,1)} %virt_hbm.1), custom_call_target="tpu_custom_call" | custom-call | tf_op jit(solution)/shard_map/pallas_call | solution.py:396
  61.6 0.8 %copy.9 = f32[1,256,512]{2,1,0:T(8,128)} copy(f32[1,256,512]{2,1,0:T(8,128)S(1)} %bitcast.1) | data formatting | bytes 1048576
  62.4 0.7 %copy.10 = f32[256,256]{1,0:T(8,128)} copy(f32[256,256]{1,0:T(8,128)S(1)} %get-tuple-element.9) | data formatting | bytes 524288

commit v4 on v3

--- a/solution.py
+++ b/solution.py
@@ -15,13 +15,14 @@
 
 
 def kernel(sizes, factor, match_hbm, mask_hbm, slab, occ_hbm, virt_hbm, pair_out, self_out, *scratch):
-    chips, orbs, reps, pieces, chunk = sizes
+    chips, orbs, reps, counts = sizes
+    pieces = len(counts)
+    firsts = [sum(counts[:c]) for c in range(pieces)]
     gath = scratch[:pieces]
     (match_ref, mask_ref, raw, masked, occ_dens, virt_dens, occ, parts, end_parts, whole, arrived, end_arrived,
      self_parts, self_whole, self_arrived, small_sem, raw_sem, dens_sem, local_sem, up_sem, down_sem,
      recv_sem, core_send, core_recv, part_send, part_recv, end_send, end_recv, self_send, self_recv) = scratch[pieces:]
     half, aux_rows, orb_cols = masked.shape
-    rows_piece = aux_rows // pieces
     rows_out = aux_rows // orbs
     self_cols = aux_rows // reps
     peers = orbs * reps
@@ -45,7 +46,7 @@
         return to_orb, {"orb": to_orb, "rep": to_rep}
 
     def rows(c):
-        return pl.ds(c * rows_piece, rows_piece)
+        return pl.ds(firsts[c], counts[c])
 
     def raw_copy(c):
         return pltpu.make_async_copy(slab.at[rows(c)], raw.at[rows(c)], raw_sem.at[c])
@@ -110,7 +111,7 @@
         return pltpu.make_async_copy(piece(c), slot(c, a), local_sem.at[c])
 
     def lower(c, send):
-        for d in range(1, chips):
+        for d in range(1, chips) if send else reversed(range(1, chips)):
             @pl.when(z - d >= 0)
             def _():
                 zz = jnp.maximum(z - d, 0)
@@ -120,7 +121,7 @@
                 cross(c, zz, slot(c, 2 * zz + k)).start()
 
     def upper(c, send):
-        for d in range(1, chips):
+        for d in range(1, chips) if send else reversed(range(1, chips)):
             @pl.when(z + d <= chips - 1)
             def _():
                 zz = jnp.minimum(z + d, chips - 1)
@@ -164,12 +165,13 @@
 
     def part_copy(c, j):
         to_orb, where = peer(j)
-        return remote(parts.at[c, j % reps, to_orb], arrived.at[c, j - 1],
+        return remote(parts.at[c, j % reps, to_orb, pl.ds(0, counts[c])], arrived.at[c, j - 1, pl.ds(0, counts[c])],
                       part_send.at[c, j - 1], part_recv.at[c, j - 1], where)
 
     def end_copy(c, j):
         to_orb, where = peer(j)
-        return remote(end_parts.at[c, j % reps, to_orb], end_arrived.at[c, j],
+        return remote(end_parts.at[c, j % reps, to_orb, pl.ds(0, counts[c])],
+                      end_arrived.at[c, j, pl.ds(0, counts[c])],
                       end_send.at[c, j], end_recv.at[c, j], dict(where, aux=end_aux))
 
     def self_copy(j):
@@ -179,8 +181,9 @@
 
     def prepare(c):
         raw_copy(c).wait()
-        for n in range(rows_piece // chunk):
-            first = c * rows_piece + n * chunk
+        chunk = min(counts[c], BLOCK // 2)
+        for n in range(counts[c] // chunk):
+            first = firsts[c] + n * chunk
             span = pl.ds(first, chunk)
             turned = pltpu.einshape("ald->lad", raw[span])
             block = first // BLOCK
@@ -206,7 +209,8 @@
         blocks = jnp.concatenate([gath[c][match_ref[(r + s) % reps, owner]] for s in range(reps)], 1)
         moved = flat_dot(blocks, virt_dens)
         total = lax.dot_general(moved, occ[which], CONTRACT, preferred_element_type=F32) * factor
-        return [[total[s * rows_piece:(s + 1) * rows_piece, q * rows_out:(q + 1) * rows_out]
+        count = counts[c]
+        return [[total[s * count:(s + 1) * count, q * rows_out:(q + 1) * rows_out]
                  for q in range(orbs)] for s in range(reps)]
 
     def gathered(c):
@@ -222,7 +226,7 @@
             tiles = turned_tiles(c, 1, end_aux)
             for s in reversed(range(reps)):
                 for q in range(orbs):
-                    end_parts[c, s, q] = tiles[s][q].astype(BF16)
+                    end_parts[c, s, q, :counts[c]] = tiles[s][q].astype(BF16)
             for j in reversed(range(peers)):
                 end_copy(c, j).start()
 
@@ -232,9 +236,9 @@
             tiles = turned_tiles(c, 0, a)
             for s in reversed(range(reps)):
                 for q in range(orbs):
-                    parts[c, s, q] = tiles[s][q].astype(BF16)
+                    parts[c, s, q, :counts[c]] = tiles[s][q].astype(BF16)
                     if s == 0:
-                        whole[c, q] = tiles[s][q]
+                        whole[c, q, :counts[c]] = tiles[s][q]
             for j in reversed(range(1, peers)):
                 part_copy(c, j).start()
 
@@ -250,15 +254,15 @@
                     self_copy(j).start()
 
     def columns(c):
-        return slice(c * rows_piece, (c + 1) * rows_piece)
+        return slice(firsts[c], firsts[c] + counts[c])
 
     def finish(c):
         @pl.when(inner)
         def _():
-            total = whole[c, o]
+            total = whole[c, o, :counts[c]]
             for j in range(1, peers):
                 part_copy(c, j).wait_recv()
-                total = total + arrived[c, j - 1].astype(F32)
+                total = total + arrived[c, j - 1, :counts[c]].astype(F32)
             pair_out[:, columns(c)] = total.T
 
     def finish_end(c):
@@ -267,7 +271,7 @@
             total = None
             for j in range(peers):
                 end_copy(c, j).wait_recv()
-                term = end_arrived[c, j].astype(F32)
+                term = end_arrived[c, j, :counts[c]].astype(F32)
                 total = term if total is None else total + term
             pair_out[:, columns(c)] = total.T
 
@@ -286,7 +290,7 @@
                 barrier,
                 peers + jnp.where(inner, 2, 1) + jnp.where(jnp.logical_or(feeds, at_end), peers - 1, 0),
             )
-        if c < 2:
+        if c < 3:
             own(c)
 
         @pl.when(inner)
@@ -305,10 +309,10 @@
         if c == 0:
             self_tiles()
     ended = 0
-    lag = 2
-    for c in range(pieces):
-        if c + 2 < pieces:
-            own(c + 2)
+    lag = 3
+    for c in range(pieces):
+        if c + 3 < pieces:
+            own(c + 3)
         if c + ahead < pieces:
             relay(c + ahead)
         filled = c + ahead >= pieces - 1
@@ -358,24 +362,44 @@
                 end_copy(c, j).wait_send()
 
 
+def write_out(pair, own, pair_out, self_out, sem):
+    copies = [pltpu.make_async_copy(src, dst, sem.at[n])
+              for n, (src, dst) in enumerate(((pair, pair_out), (own, self_out)))]
+    for copy in copies:
+        copy.start()
+    for copy in copies:
+        copy.wait()
+
+
+def store(pair, own):
+    return pl.pallas_call(
+        write_out,
+        out_shape=(jax.ShapeDtypeStruct(pair.shape, F32), jax.ShapeDtypeStruct(own.shape, F32)),
+        in_specs=[pl.BlockSpec(memory_space=pltpu.VMEM)] * 2,
+        out_specs=(pl.BlockSpec(memory_space=pltpu.HBM),) * 2,
+        scratch_shapes=[pltpu.SemaphoreType.DMA((2,))],
+        compiler_params=pltpu.CompilerParams(vmem_limit_bytes=4 * 2**20),
+    )(pair, own)
+
+
 def per_device(slab, occ_density, virt_density, block_mask, matching):
     owners = lax.axis_size("aux")
     orbs = lax.axis_size("orb")
     reps = lax.axis_size("rep")
     chips = owners // 2
     aux_rows, batch, orb_cols = slab.shape
-    pieces = max(2, 32 // chips)
-    rows_piece = aux_rows // pieces
+    rows_piece = aux_rows // max(2, 32 // chips)
+    counts = (rows_piece,) * (aux_rows // rows_piece)
+    pieces = len(counts)
     half = batch // reps
     rows_out = aux_rows // orbs
     self_cols = aux_rows // reps
     peers = orbs * reps
-    chunk = min(rows_piece, BLOCK // 2)
     factor = 1.0 / math.sqrt(batch * orb_cols * orbs)
     dma = pltpu.SemaphoreType.DMA
     vmem = pl.BlockSpec(memory_space=pltpu.VMEM)
     hbm = pl.BlockSpec(memory_space=pltpu.HBM)
-    gathers = [pltpu.VMEM((owners, half, rows_piece, orb_cols), BF16) for _ in range(pieces)]
+    gathers = [pltpu.VMEM((owners, half, count, orb_cols), BF16) for count in counts]
     buffers = [
         ((aux_rows, batch, orb_cols), BF16),
         ((half, aux_rows, orb_cols), BF16),
@@ -394,7 +418,7 @@
     held = sum(math.prod(shape) * jnp.dtype(kind).itemsize for shape, kind in buffers)
     held += owners * half * aux_rows * orb_cols * jnp.dtype(BF16).itemsize
     pair, own = pl.pallas_call(
-        functools.partial(kernel, (chips, orbs, reps, pieces, chunk), factor),
+        functools.partial(kernel, (chips, orbs, reps, counts), factor),
         out_shape=(
             jax.ShapeDtypeStruct((rows_out, aux_rows), F32),
             jax.ShapeDtypeStruct((rows_out, self_cols), F32),
@@ -415,7 +439,7 @@
         ),
     )(*(pltpu.with_memory_space_constraint(x, pltpu.HBM)
         for x in (matching, block_mask, slab, occ_density, virt_density)))
-    return (pair[None], own)
+    return store(pair[None], own)
 
 
 def solution(mesh):

time: 63.2 us -> 62.6 us (level)
  local copies, waits for them, and re-layouts: 1.5 us -> 0 us
  Pallas kernels: 60.9 us -> 61.8 us
    unnamed x2 -> x0, local copies, waits for them, and re-layouts: 1.5 us -> none
    pallas_call x1 -> x2, Pallas kernels: 60.9 us -> 61.8 us  [the longest x1 60.9 us: per_device(): pl.pallas_call(functools.partial(kernel, (chips, orbs, reps, counts), fac...]
where the time goes in v4:
time: 62.6 us; the launch traced here: 62.5 us
  Pallas kernels  61.8 us (99%)
  between operations  0.64 us (1%)
    pallas_call x1, Pallas kernels, per_device(): pl.pallas_call(functools.partial(kernel, (chips, orbs, reps, counts), fac...  60.9 us

profile of v4, /device:TPU:1, one launch (start us, length us, event | category | flops | bytes accessed | tf_op | source)
XLA Modules:
  0.0 62.5 jit_solution(5623930716336105619)
XLA Ops:
  0.6 60.9 %shard_map.68 = (f32[256,512]{1,0:T(8,128)S(1)}, f32[256,256]{1,0:T(8,128)S(1)}) custom-call(s32[2,8]{1,0:T(2,128)} %match_hbm.1, s32[4,4]{1,0:T(4,128)} %mask_hbm.1, bf16[512,4,512]{2,1,0:T(4,128)(2,1)} %slab.1, bf16[512,512]{1,0:T(8,128)(2,1)} %occ_hbm.1, bf16[512,512]{1,0:T(8,128)(2,1)} %virt_hbm.1), custom_call_target="tpu_custom_call" | custom-call | tf_op jit(solution)/shard_map/pallas_call | solution.py:420
  61.6 0.9 %shard_map.69 = (f32[1,256,512]{2,1,0:T(8,128)}, f32[256,256]{1,0:T(8,128)}) custom-call(f32[1,256,512]{2,1,0:T(8,128)S(1)} %bitcast.1, f32[256,256]{1,0:T(8,128)S(1)} %get-tuple-element.5.own), custom_call_target="tpu_custom_call" | custom-call | tf_op jit(solution)/shard_map/pallas_call | solution.py:375
